TPU v7x, 256 devices: a whole 4x4x8 slice. The times are simulated.
256 devices in a mesh: slot: 8 (over y, core), asset: 32 (over x, z).
Axes of the slice: x: 4, y: 4, z: 8, core: 2. Of those that a mesh axis runs over, the one named last changes fastest.
Arguments:
- slot_emb: bfloat16 [16384, 768], P(('slot', 'asset')), may hold values from -4 to 4
- asset_panel: bfloat16 [768, 32768], P('slot', 'asset'), may hold values from -4 to 4
- mult: int32 [16384], P('slot'), may hold values from 1 to 4
- caps: int32 [32768], P('asset'), may hold values from 1 to 8, as said below
Outputs:
- plan: float32 [16384, 32768], P('slot', 'asset')
Inputs may be any that keep to these rules, and one draw needn't show every extreme that they name: caps are whole numbers; the last asset's cap is the largest.
All inputs are finite; a program needn't handle non-finite values.
Results may differ from a plain program's by a relative error of at most 0.0003.
Values may be sent and summed in bfloat16 or wider, within the bound.
No kernel may reach another device: no remote copies, remote signals or barrier semaphores. Data moves between devices by JAX's collectives and lax.ppermute only.
A program may use at most 64 MiB of HBM per device.

v0:
```python
import jax
import jax.numpy as jnp
from jax import lax
from jax.sharding import PartitionSpec as P

EMB = 768
ITERS = 3


def row_side(logits, asset_pot):
    shifted = logits + asset_pot[None, :]
    peak = lax.pmax(jnp.max(shifted, axis=1), "asset")
    total = lax.psum(jnp.sum(jnp.exp(shifted - peak[:, None]), axis=1), "asset")
    return peak + jnp.log(total)


def col_side(logits, slot_pot):
    shifted = logits + slot_pot[:, None]
    peak = lax.pmax(jnp.max(shifted, axis=0), "slot")
    total = lax.psum(jnp.sum(jnp.exp(shifted - peak[None, :]), axis=0), "slot")
    return peak + jnp.log(total)


def per_device(slot_emb, asset_panel, mult, caps):
    slot_block = lax.all_gather(slot_emb, "asset", axis=0, tiled=True)
    logits = jnp.dot(
        slot_block,
        lax.all_gather(asset_panel, "slot", axis=0, tiled=True),
        preferred_element_type=jnp.float32,
    ) * EMB ** (-0.5)
    caps_float = caps.astype(jnp.float32)
    cap_total = lax.psum(jnp.sum(caps_float), "asset")
    log_b = jnp.log(caps_float) - jnp.log(cap_total)
    log_a = jnp.log(mult.astype(jnp.float32))
    asset_pot = jnp.zeros((logits.shape[1],), jnp.float32)
    slot_pot = jnp.zeros((logits.shape[0],), jnp.float32)
    for iteration in range(ITERS):
        slot_pot = log_a - row_side(logits, asset_pot)
        asset_pot = log_b - col_side(logits, slot_pot)
    factor = float(
        logits.shape[0] * lax.axis_size("slot") * logits.shape[1] * lax.axis_size("asset")
    )
    return jnp.exp(logits + slot_pot[:, None] + asset_pot[None, :]) * factor


def solution(mesh):
    return jax.shard_map(
        per_device,
        mesh=mesh,
        in_specs=(P(("slot", "asset"), None), P("slot", "asset"), P("slot"), P("asset")),
        out_specs=P("slot", "asset"),
        check_vma=False,
    )
```

profile of v0, /device:TPU:1, one launch (start us, length us, event | category | flops | bytes accessed | tf_op | source)
XLA Modules:
  0.0 697.3 jit_solution(16595806168147780768)
XLA Ops:
  6.5 0.7 all-gather.5.cloned.1.call-update
  7.3 0.0 all-gather.3.cloned.1.call-start
  7.3 0.7 all-gather.3.cloned.1.call-update
  8.0 1.3 convert_reduce_fusion
  9.3 31.0 %all-gather.5.cloned.1.call-done = bf16[768,1024]{1,0:T(8,128)(2,1)} async-done(((bf16[96,1024]{1,0:T(8,128)(2,1)}), bf16[768,1024]{1,0:T(8,128)(2,1)}) %all-gather.5.cloned.1.call-update) | async-done | bytes 1572880 | tf_op jit(solution)/shard_map/all_gather | solution.py:28
  40.3 77.9 %all-gather.3.cloned.1.call-done = bf16[2048,768]{1,0:T(8,128)(2,1)} async-done(((bf16[64,768]{1,0:T(8,128)(2,1)}), bf16[2048,768]{1,0:T(8,128)(2,1)}) %all-gather.3.cloned.1.call-update) | async-done | bytes 3145744 | tf_op jit(solution)/shard_map/all_gather | solution.py:25
  118.2 9.2 %fusion = (f32[2048]{0:T(1024)S(1)}, f32[2048,1024]{1,0:T(8,128)}) fusion(bf16[2048,768]{1,0:T(8,128)(2,1)} %all-gather.3.cloned.1.call-done, bf16[768,1024]{1,0:T(8,128)(2,1)} %all-gather.5.cloned.1.call-done), kind=kOutput, calls=%fused_computation.22 | convolution fusion | flops 3225417728 | bytes 13115392 | tf_op jit(solution)/shard_map/dot_general | solution.py:26
  127.4 58.9 %pmax.42 = f32[2048]{0:T(1024)S(1)} all-reduce(f32[2048]{0:T(1024)S(1)} %get-tuple-element.7), channel_id=1, replica_groups=mesh['slot'=8,'asset'=32] {'asset'}, use_global_device_ids=true, to_apply=%region_3.0 | all-reduce | flops 2048 | bytes 16384 | tf_op jit(solution)/shard_map/pmax | solution.py:12
  186.3 4.4 exponential_reduce_fusion.5
  190.7 58.3 %all-reduce = (f32[2048]{0:T(1024)S(1)}, f32[]{:T(128)}) all-reduce(f32[2048]{0:T(1024)S(1)} %exponential_reduce_fusion.5, f32[]{:T(128)} %convert_reduce_fusion), channel_id=1, replica_groups=mesh['slot'=8,'asset'=32] {'asset'}, use_global_device_ids=true, to_apply=%region_5.0 | all-reduce | flops 2049 | bytes 16392 | tf_op jit(solution)/shard_map/psum | solution.py:13
  249.6 0.0 copy-start.1
  249.6 4.0 add_reduce_fusion.3
  253.6 44.0 %pmax.43 = f32[1024]{0:T(1024)S(1)} all-reduce(f32[1024]{0:T(1024)S(1)} %add_reduce_fusion.3), channel_id=1, replica_groups=mesh['slot'=8,'asset'=32] {'slot'}, use_global_device_ids=true, to_apply=%region_7.0 | all-reduce | flops 1024 | bytes 8192 | tf_op jit(solution)/shard_map/pmax | solution.py:19
  297.6 4.2 exponential_reduce_fusion.4
  301.9 12.4 %psum.51 = f32[1024]{0:T(1024)S(1)} all-reduce(f32[1024]{0:T(1024)S(1)} %exponential_reduce_fusion.4), channel_id=1, replica_groups=mesh['slot'=8,'asset'=32] {'slot'}, use_global_device_ids=true, to_apply=%region_9.0 | all-reduce | flops 1024 | bytes 8192 | tf_op jit(solution)/shard_map/psum | solution.py:20
  314.3 4.0 add_reduce_fusion.2
  318.3 59.1 %pmax.44 = f32[2048]{0:T(1024)S(1)} all-reduce(f32[2048]{0:T(1024)S(1)} %add_reduce_fusion.2), channel_id=1, replica_groups=mesh['slot'=8,'asset'=32] {'asset'}, use_global_device_ids=true, to_apply=%region_11.0 | all-reduce | flops 2048 | bytes 16384 | tf_op jit(solution)/shard_map/pmax | solution.py:12
  377.5 4.4 exponential_reduce_fusion.3
  381.8 57.1 %psum.52 = f32[2048]{0:T(1024)S(1)} all-reduce(f32[2048]{0:T(1024)S(1)} %exponential_reduce_fusion.3), channel_id=1, replica_groups=mesh['slot'=8,'asset'=32] {'asset'}, use_global_device_ids=true, to_apply=%region_13.0 | all-reduce | flops 2048 | bytes 16384 | tf_op jit(solution)/shard_map/psum | solution.py:13
  438.9 4.0 add_reduce_fusion.1
  442.9 39.6 %pmax.45 = f32[1024]{0:T(1024)S(1)} all-reduce(f32[1024]{0:T(1024)S(1)} %add_reduce_fusion.1), channel_id=1, replica_groups=mesh['slot'=8,'asset'=32] {'slot'}, use_global_device_ids=true, to_apply=%region_15.0 | all-reduce | flops 1024 | bytes 8192 | tf_op jit(solution)/shard_map/pmax | solution.py:19
  482.5 4.2 exponential_reduce_fusion.2
  486.8 12.4 %psum.53 = f32[1024]{0:T(1024)S(1)} all-reduce(f32[1024]{0:T(1024)S(1)} %exponential_reduce_fusion.2), channel_id=1, replica_groups=mesh['slot'=8,'asset'=32] {'slot'}, use_global_device_ids=true, to_apply=%region_17.0 | all-reduce | flops 1024 | bytes 8192 | tf_op jit(solution)/shard_map/psum | solution.py:20
  499.2 4.0 add_reduce_fusion
  503.2 59.2 %pmax.46 = f32[2048]{0:T(1024)S(1)} all-reduce(f32[2048]{0:T(1024)S(1)} %add_reduce_fusion), channel_id=1, replica_groups=mesh['slot'=8,'asset'=32] {'asset'}, use_global_device_ids=true, to_apply=%region_19.0 | all-reduce | flops 2048 | bytes 16384 | tf_op jit(solution)/shard_map/pmax | solution.py:12
  562.4 4.4 exponential_reduce_fusion.1
  566.7 57.0 %psum.54 = f32[2048]{0:T(1024)S(1)} all-reduce(f32[2048]{0:T(1024)S(1)} %exponential_reduce_fusion.1), channel_id=1, replica_groups=mesh['slot'=8,'asset'=32] {'asset'}, use_global_device_ids=true, to_apply=%region_21.0 | all-reduce | flops 2048 | bytes 16384 | tf_op jit(solution)/shard_map/psum | solution.py:13
  623.8 4.0 add_reduce_fusion.4
  627.8 39.6 %pmax.47 = f32[1024]{0:T(1024)S(1)} all-reduce(f32[1024]{0:T(1024)S(1)} %add_reduce_fusion.4), channel_id=1, replica_groups=mesh['slot'=8,'asset'=32] {'slot'}, use_global_device_ids=true, to_apply=%region_23.0 | all-reduce | flops 1024 | bytes 8192 | tf_op jit(solution)/shard_map/pmax | solution.py:19
  667.4 4.2 exponential_reduce_fusion
  671.7 12.4 %psum.55 = f32[1024]{0:T(1024)S(1)} all-reduce(f32[1024]{0:T(1024)S(1)} %exponential_reduce_fusion), channel_id=1, replica_groups=mesh['slot'=8,'asset'=32] {'slot'}, use_global_device_ids=true, to_apply=%region_25.0 | all-reduce | flops 1024 | bytes 8192 | tf_op jit(solution)/shard_map/psum | solution.py:20
  684.1 6.3 exponential_multiply_fusion
  (10 shorter events, 0.1 us)
Async XLA Ops:
  6.5 33.7 %all-gather.5.cloned.1.call-start = ((), (), s32[]{:S(2)}) async-start(), calls=%async_computation.1 | async-start | bytes 1769472 | tf_op jit(solution)/shard_map/all_gather | solution.py:28
  7.3 110.9 %all-gather.3.cloned.1.call-start = ((), (), s32[]{:S(2)}) async-start(), calls=%async_computation | async-start | bytes 3244032 | tf_op jit(solution)/shard_map/all_gather | solution.py:25
  127.4 122.2 %copy-start = (s32[2048]{0:T(1024)S(1)}, s32[2048]{0:T(1024)}, u32[]{:S(2)}) copy-start(s32[2048]{0:T(1024)} %param.6) | copy-start | bytes 24580
  249.6 64.7 %copy-start.1 = (s32[1024]{0:T(1024)S(1)}, s32[1024]{0:T(1024)}, u32[]{:S(2)}) copy-start(s32[1024]{0:T(1024)} %param.7) | copy-start | bytes 12292
Sparse Core Ops, SparseCore 0:
  9.2 31.0 all-gather.4
  42.8 75.2 all-gather.2
where the time goes:
time: 698 us; the launch traced here: 697 us
  blocking collectives  510 us (73%)
  waiting for transfers between devices  110 us (16%)
  other arithmetic  53.5 us (8%)
  between operations  14.2 us (2%)
  matrix products  9.19 us (1%)
    pmax x3, blocking collectives, row_side(): peak = lax.pmax(jnp.max(shifted, axis=1), 'asset')  177 us
    psum x3, blocking collectives, row_side(): total = lax.psum(jnp.sum(jnp.exp(shifted - peak[:, None]), axis=1), 'asset')  172 us
    pmax x3, blocking collectives, col_side(): peak = lax.pmax(jnp.max(shifted, axis=0), 'slot')  123 us
    all_gather x1, waiting for transfers between devices, per_device(): slot_block = lax.all_gather(slot_emb, 'asset', axis=0, tiled=True)  77.9 us
    psum x3, blocking collectives, col_side(): total = lax.psum(jnp.sum(jnp.exp(shifted - peak[None, :]), axis=0), 'slot')  37.3 us
    all_gather x1, waiting for transfers between devices, per_device(): lax.all_gather(asset_panel, 'slot', axis=0, tiled=True)  31 us
  transfers between devices with their start and end apart: 2, of which 2 were waited for; matrix products, arithmetic and copies ran while one was open for 0% of the time, Pallas kernels for 0%

commit v1 on v0

--- a/solution.py
+++ b/solution.py
@@ -10,7 +10,9 @@
 def row_side(logits, asset_pot):
     shifted = logits + asset_pot[None, :]
     peak = lax.pmax(jnp.max(shifted, axis=1), "asset")
-    total = lax.psum(jnp.sum(jnp.exp(shifted - peak[:, None]), axis=1), "asset")
+    total = jnp.sum(
+        lax.all_gather(jnp.sum(jnp.exp(shifted - peak[:, None]), axis=1), "asset"), axis=0
+    )
     return peak + jnp.log(total)
 
 

time: 698 us -> 624 us (0.89)
  waiting for transfers between devices: 110 us -> 44.6 us
  blocking collectives: 510 us -> 501 us
    psum x3 -> x1, blocking collectives: 172 us -> 65 us  [per_device(): cap_total = lax.psum(jnp.sum(caps_float), 'asset')]
    all_gather x0 -> x3, blocking collectives: none -> 103 us  [row_side(): lax.all_gather(jnp.sum(jnp.exp(shifted - peak[:, None]), axis=1), 'asset')]
    all_gather x1, waiting for transfers between devices: 77.9 us -> 43.2 us  [per_device(): slot_block = lax.all_gather(slot_emb, 'asset', axis=0, tiled=True)]
    all_gather x1, waiting for transfers between devices: 31 us -> 0.02 us  [per_device(): lax.all_gather(asset_panel, 'slot', axis=0, tiled=True)]
  transfers between devices with their start and end apart: 2 -> 2, of which waited for: 2 -> 1; matrix products, arithmetic and copies ran while one was open for 0% -> 0% of each run, Pallas kernels for 0% -> 0%
where the time goes in v1:
time: 624 us; the launch traced here: 623 us
  blocking collectives  501 us (80%)
  other arithmetic  53.6 us (9%)
  waiting for transfers between devices  44.6 us (7%)
  between operations  14.3 us (2%)
  matrix products  9.19 us (1%)
    pmax x3, blocking collectives, row_side(): peak = lax.pmax(jnp.max(shifted, axis=1), 'asset')  177 us
    pmax x3, blocking collectives, col_side(): peak = lax.pmax(jnp.max(shifted, axis=0), 'slot')  119 us
    all_gather x3, blocking collectives, row_side(): lax.all_gather(jnp.sum(jnp.exp(shifted - peak[:, None]), axis=1), 'asset')  103 us
    psum x1, blocking collectives, per_device(): cap_total = lax.psum(jnp.sum(caps_float), 'asset')  65 us
    all_gather x1, waiting for transfers between devices, per_device(): slot_block = lax.all_gather(slot_emb, 'asset', axis=0, tiled=True)  43.2 us
    psum x3, blocking collectives, col_side(): total = lax.psum(jnp.sum(jnp.exp(shifted - peak[None, :]), axis=0), 'slot')  37.3 us
    reduce_sum x3, other arithmetic, row_side(): jnp.sum(jnp.exp(shifted - peak[:, None]), axis=1)  13.1 us
    reduce_sum x3, other arithmetic, col_side(): total = lax.psum(jnp.sum(jnp.exp(shifted - peak[None, :]), axis=0), 'slot')  12.7 us
  transfers between devices with their start and end apart: 2, of which 1 were waited for; matrix products, arithmetic and copies ran while one was open for 0% of the time, Pallas kernels for 0%

profile of v1, /device:TPU:1, one launch (start us, length us, event | category | flops | bytes accessed | tf_op | source)
XLA Modules:
  0.0 623.1 jit_solution(16454360630567004991)
XLA Ops:
  6.5 0.7 all-gather.8.cloned.1.call-update
  7.3 0.0 all-gather.6.cloned.1.call-start
  7.3 0.7 all-gather.6.cloned.1.call-update
  8.0 1.3 convert_reduce_fusion
  9.3 65.0 %psum.28 = f32[]{:T(128)} all-reduce(f32[]{:T(128)} %convert_reduce_fusion), channel_id=1, replica_groups=mesh['slot'=8,'asset'=32] {'asset'}, use_global_device_ids=true, to_apply=%region_1.0 | all-reduce | flops 1 | bytes 8 | tf_op jit(solution)/shard_map/psum | solution.py:34
  75.0 0.0 all-gather.8.cloned.1.call-done
  75.0 43.2 %all-gather.6.cloned.1.call-done = bf16[2048,768]{1,0:T(8,128)(2,1)} async-done(((bf16[64,768]{1,0:T(8,128)(2,1)}), bf16[2048,768]{1,0:T(8,128)(2,1)}) %all-gather.6.cloned.1.call-update) | async-done | bytes 3145744 | tf_op jit(solution)/shard_map/all_gather | solution.py:27
  118.2 9.2 %fusion = (f32[2048]{0:T(1024)S(1)}, f32[2048,1024]{1,0:T(8,128)}) fusion(bf16[2048,768]{1,0:T(8,128)(2,1)} %all-gather.6.cloned.1.call-done, bf16[768,1024]{1,0:T(8,128)(2,1)} %all-gather.8.cloned.1.call-done), kind=kOutput, calls=%fused_computation.22 | convolution fusion | flops 3225417728 | bytes 13115392 | tf_op jit(solution)/shard_map/dot_general | solution.py:28
  127.4 58.9 %pmax.42 = f32[2048]{0:T(1024)S(1)} all-reduce(f32[2048]{0:T(1024)S(1)} %get-tuple-element.5), channel_id=1, replica_groups=mesh['slot'=8,'asset'=32] {'asset'}, use_global_device_ids=true, to_apply=%region_3.0 | all-reduce | flops 2048 | bytes 16384 | tf_op jit(solution)/shard_map/pmax | solution.py:12
  186.3 4.4 exponential_reduce_fusion.5
  190.7 34.4 %all-gather = f32[65536]{0:T(1024)S(1)} all-gather(f32[2048]{0:T(1024)S(1)} %exponential_reduce_fusion.5), channel_id=2, replica_groups=mesh['slot'=8,'asset'=32] {'asset'}, dimensions={0}, use_global_device_ids=true | all-gather | bytes 270336 | tf_op jit(solution)/shard_map/all_gather | solution.py:14
  225.2 4.0 add_reduce_fusion.3
  229.2 41.9 %pmax.43 = f32[1024]{0:T(1024)S(1)} all-reduce(f32[1024]{0:T(1024)S(1)} %add_reduce_fusion.3), channel_id=1, replica_groups=mesh['slot'=8,'asset'=32] {'slot'}, use_global_device_ids=true, to_apply=%region_7.0 | all-reduce | flops 1024 | bytes 8192 | tf_op jit(solution)/shard_map/pmax | solution.py:21
  271.1 4.2 exponential_reduce_fusion.4
  275.3 12.4 %psum.29 = f32[1024]{0:T(1024)S(1)} all-reduce(f32[1024]{0:T(1024)S(1)} %exponential_reduce_fusion.4), channel_id=1, replica_groups=mesh['slot'=8,'asset'=32] {'slot'}, use_global_device_ids=true, to_apply=%region_9.0 | all-reduce | flops 1024 | bytes 8192 | tf_op jit(solution)/shard_map/psum | solution.py:22
  287.8 4.0 add_reduce_fusion.2
  291.8 59.1 %pmax.44 = f32[2048]{0:T(1024)S(1)} all-reduce(f32[2048]{0:T(1024)S(1)} %add_reduce_fusion.2), channel_id=1, replica_groups=mesh['slot'=8,'asset'=32] {'asset'}, use_global_device_ids=true, to_apply=%region_11.0 | all-reduce | flops 2048 | bytes 16384 | tf_op jit(solution)/shard_map/pmax | solution.py:12
  350.9 4.4 exponential_reduce_fusion.3
  355.3 34.2 %all-gather.1 = f32[65536]{0:T(1024)S(1)} all-gather(f32[2048]{0:T(1024)S(1)} %exponential_reduce_fusion.3), channel_id=3, replica_groups=mesh['slot'=8,'asset'=32] {'asset'}, dimensions={0}, use_global_device_ids=true | all-gather | bytes 270336 | tf_op jit(solution)/shard_map/all_gather | solution.py:14
  389.6 4.0 add_reduce_fusion.1
  393.6 38.4 %pmax.45 = f32[1024]{0:T(1024)S(1)} all-reduce(f32[1024]{0:T(1024)S(1)} %add_reduce_fusion.1), channel_id=1, replica_groups=mesh['slot'=8,'asset'=32] {'slot'}, use_global_device_ids=true, to_apply=%region_15.0 | all-reduce | flops 1024 | bytes 8192 | tf_op jit(solution)/shard_map/pmax | solution.py:21
  432.1 4.2 exponential_reduce_fusion.2
  436.3 12.4 %psum.30 = f32[1024]{0:T(1024)S(1)} all-reduce(f32[1024]{0:T(1024)S(1)} %exponential_reduce_fusion.2), channel_id=1, replica_groups=mesh['slot'=8,'asset'=32] {'slot'}, use_global_device_ids=true, to_apply=%region_17.0 | all-reduce | flops 1024 | bytes 8192 | tf_op jit(solution)/shard_map/psum | solution.py:22
  448.7 4.0 add_reduce_fusion
  452.8 59.3 %pmax.46 = f32[2048]{0:T(1024)S(1)} all-reduce(f32[2048]{0:T(1024)S(1)} %add_reduce_fusion), channel_id=1, replica_groups=mesh['slot'=8,'asset'=32] {'asset'}, use_global_device_ids=true, to_apply=%region_19.0 | all-reduce | flops 2048 | bytes 16384 | tf_op jit(solution)/shard_map/pmax | solution.py:12
  512.1 4.4 exponential_reduce_fusion.1
  516.4 34.2 %all-gather.2 = f32[65536]{0:T(1024)S(1)} all-gather(f32[2048]{0:T(1024)S(1)} %exponential_reduce_fusion.1), channel_id=4, replica_groups=mesh['slot'=8,'asset'=32] {'asset'}, dimensions={0}, use_global_device_ids=true | all-gather | bytes 270336 | tf_op jit(solution)/shard_map/all_gather | solution.py:14
  550.8 4.0 add_reduce_fusion.4
  554.8 38.4 %pmax.47 = f32[1024]{0:T(1024)S(1)} all-reduce(f32[1024]{0:T(1024)S(1)} %add_reduce_fusion.4), channel_id=1, replica_groups=mesh['slot'=8,'asset'=32] {'slot'}, use_global_device_ids=true, to_apply=%region_23.0 | all-reduce | flops 1024 | bytes 8192 | tf_op jit(solution)/shard_map/pmax | solution.py:21
  593.2 4.2 exponential_reduce_fusion
  597.5 12.4 %psum.31 = f32[1024]{0:T(1024)S(1)} all-reduce(f32[1024]{0:T(1024)S(1)} %exponential_reduce_fusion), channel_id=1, replica_groups=mesh['slot'=8,'asset'=32] {'slot'}, use_global_device_ids=true, to_apply=%region_25.0 | all-reduce | flops 1024 | bytes 8192 | tf_op jit(solution)/shard_map/psum | solution.py:22
  609.9 6.3 %exponential_multiply_fusion = f32[2048,1024]{1,0:T(8,128)} fusion(f32[2048,1024]{1,0:T(8,128)} %get-tuple-element.6, f32[1024]{0:T(1024)S(1)} %add_subtract_fusion.3, f32[2048]{0:T(1024)S(1)} %add_subtract_fusion), kind=kLoop, calls=%fused_computation | loop fusion | flops 6291456 | bytes 16789504 | tf_op jit(solution)/shard_map/mul | solution.py:45
  (17 shorter events, 0.3 us)
Async XLA Ops:
  6.5 68.5 %all-gather.8.cloned.1.call-start = ((), (), s32[]{:S(2)}) async-start(), calls=%async_computation.1 | async-start | bytes 1769472 | tf_op jit(solution)/shard_map/all_gather | solution.py:30
  7.3 110.9 %all-gather.6.cloned.1.call-start = ((), (), s32[]{:S(2)}) async-start(), calls=%async_computation | async-start | bytes 3244032 | tf_op jit(solution)/shard_map/all_gather | solution.py:27
  127.4 97.8 %copy-start = (s32[2048]{0:T(1024)S(1)}, s32[2048]{0:T(1024)}, u32[]{:S(2)}) copy-start(s32[2048]{0:T(1024)} %param.6) | copy-start | bytes 24580
  225.2 62.6 %copy-start.1 = (s32[1024]{0:T(1024)S(1)}, s32[1024]{0:T(1024)}, u32[]{:S(2)}) copy-start(s32[1024]{0:T(1024)} %param.7) | copy-start | bytes 12292
Sparse Core Ops, SparseCore 0:
  9.2 31.0 all-gather.7
  42.8 75.2 all-gather.5
